TPU v7x, 32 devices: a whole 2x2x4 slice. The times are simulated.
32 devices in a mesh: shard: 4 (over z), tensor: 4 (over x, core), section: 2 (over y).
Axes of the slice: x: 2, y: 2, z: 4, core: 2. Of those that a mesh axis runs over, the one named last changes fastest.
Arguments:
- hidden_acts: bfloat16 [2, 10240, 4096], P('section', 'shard', 'tensor'), may hold values from -8 to 8
- out_grads: bfloat16 [2, 10240, 1024], P('section', 'shard'), may hold values from -8 to 8
- errors: float32 [2, 4, 1024, 4096], P('section', 'shard', None, 'tensor'), may hold values from -3 to 3
- factors: float32 [2, 32, 4096], P('section', None, 'tensor'), may hold values from -6 to 6
- whiten: float32 [2, 2, 32, 32], P('section'), may hold values from -1.5 to 3
- momentum: float32 [2, 1024, 4096], P('section', 'shard', 'tensor'), may hold values from -3 to 3
- master: float32 [2, 1024, 4096], P('section', 'shard', 'tensor'), may hold values from -3 to 3
- table: bfloat16 [32768, 1024], P(('shard', 'section'), 'tensor'), may hold values from -5 to 5
- touched_ids: int32 [1024], P(('shard', 'section')), may hold values from 0 to 32767, as said below
- touched_grads: bfloat16 [1024, 1024], P(('shard', 'section'), 'tensor'), may hold values from -5 to 5
Outputs:
- new_errors: float32 [2, 4, 1024, 4096], P('section', 'shard', None, 'tensor')
- new_factors: float32 [2, 32, 4096], P('section', None, 'tensor')
- new_momentum: float32 [2, 1024, 4096], P('section', 'shard', 'tensor')
- new_master: float32 [2, 1024, 4096], P('section', 'shard', 'tensor')
- new_weights: bfloat16 [2, 1024, 4096], P('section', None, 'tensor')
- new_table: bfloat16 [32768, 1024], P(('shard', 'section'), 'tensor')
Inputs may be any that keep to these rules, and one draw needn't show every extreme that they name: `touched_ids`: the 128 ids of one device of shard and section name at most 32 rows in each block of 4096 vocabulary rows; in every draw one block receives exactly 32 rows from every device.
All inputs are finite; a program needn't handle non-finite values.
Results may differ from a plain program's by a relative error of at most 0.0036.
Values may be sent and summed in bfloat16 or wider, within the bound.
A program may use at most 128 MiB of HBM per device.

v0:
```python
import jax
import jax.numpy as jnp
from jax import lax
from jax.sharding import PartitionSpec as P

D = 1024
FF = 4096
ROUNDS = 2
epsilon = 1e-06
momentum_decay = 0.9
learn_rate = 0.1
embed_rate = 0.25
clip_level = 0.03
highest = lax.Precision.HIGHEST


def on_device(
    hidden_acts,
    out_grads,
    errors,
    factors,
    whiten,
    momentum,
    master,
    table,
    touched_ids,
    touched_grads,
):
    shards = lax.axis_size("shard")
    grad_block = lax.dot_general(
        out_grads[0], hidden_acts[0], (((0,), (0,)), ((), ())), preferred_element_type=jnp.float32
    )
    rounded = lax.optimization_barrier(grad_block.astype(jnp.bfloat16))
    corrected = rounded.astype(jnp.float32) + errors[0, 0]
    right_part = factors[0]
    rank_count = right_part.shape[0]
    left_unit = None
    for power_round in range(ROUNDS):
        left_part = lax.dot_general(
            right_part,
            corrected,
            (((1,), (1,)), ((), ())),
            precision=highest,
            preferred_element_type=jnp.float32,
        )
        left_sum = lax.psum(left_part, ("shard", "tensor"))
        whitened = jnp.dot(whiten[0, power_round].T, left_sum, precision=highest)
        scaling = lax.rsqrt(jnp.sum(whitened * whitened) / rank_count + epsilon)
        left_unit = whitened * scaling
        right_local = jnp.dot(left_unit, corrected, precision=highest)
        right_part = lax.psum(right_local, "shard") / shards
    gram_left = jnp.dot(left_unit, left_unit.T, precision=highest)
    gram_right = jnp.dot(right_part, right_part.T, precision=highest)
    total_squares = lax.psum(jnp.sum(gram_left * gram_right), ("tensor", "section"))
    approx = lax.dot_general(
        left_unit,
        right_part,
        (((0,), (0,)), ((), ())),
        precision=highest,
        preferred_element_type=jnp.float32,
    )
    new_errors = (corrected - approx)[None, None]
    entries = lax.axis_size("section") * D * FF
    spread = jnp.sqrt(total_squares / entries + epsilon)
    clip_factor = jnp.minimum(1.0, clip_level / spread)
    rows_own = momentum.shape[1]
    row_start = lax.axis_index("shard") * rows_own
    approx_rows = lax.dynamic_slice_in_dim(approx, row_start, rows_own, 0)
    new_momentum = momentum_decay * momentum + clip_factor * approx_rows[None]
    new_master = master - learn_rate * new_momentum
    new_weights = lax.all_gather(new_master.astype(jnp.bfloat16), "shard", axis=1, tiled=True)
    new_factors = right_part[None]
    vocab_rows = table.shape[0]
    table_width = table.shape[1]
    first_row = lax.axis_index(("shard", "section")) * vocab_rows
    recv_rows, recv_ids = (
        lax.all_gather(touched_grads, ("shard", "section"), axis=0, tiled=True),
        lax.all_gather(touched_ids, ("shard", "section"), axis=0, tiled=True),
    )
    local_index = recv_ids - first_row
    inside = (local_index >= 0) & (local_index < vocab_rows)
    target = jnp.where(inside, local_index, vocab_rows)
    table_grad = (
        jnp.zeros((vocab_rows, table_width), jnp.float32)
        .at[target]
        .add(recv_rows.astype(jnp.float32), mode="drop")
    )
    new_table = (table.astype(jnp.float32) - embed_rate * table_grad).astype(jnp.bfloat16)
    return (new_errors, new_factors, new_momentum, new_master, new_weights, new_table)


def solution(mesh):
    in_specs = (
        P("section", "shard", "tensor"),
        P("section", "shard", None),
        P("section", "shard", None, "tensor"),
        P("section", None, "tensor"),
        P("section", None, None, None),
        P("section", "shard", "tensor"),
        P("section", "shard", "tensor"),
        P(("shard", "section"), "tensor"),
        P(("shard", "section")),
        P(("shard", "section"), "tensor"),
    )
    out_specs = (
        P("section", "shard", None, "tensor"),
        P("section", None, "tensor"),
        P("section", "shard", "tensor"),
        P("section", "shard", "tensor"),
        P("section", None, "tensor"),
        P(("shard", "section"), "tensor"),
    )
    return jax.shard_map(
        on_device, mesh=mesh, in_specs=in_specs, out_specs=out_specs, check_vma=False
    )
```

profile of v0, /device:TPU:0, one launch (start us, length us, event | category | flops | bytes accessed | tf_op | source)
XLA Modules:
  0.0 398.0 jit_solution(17824651592674097183)
XLA Ops:
  7.2 0.0 all-reduce.5.cloned.1.call-start
  7.2 9.3 %fusion.5 = bf16[1024,1024]{1,0:T(8,128)(2,1)S(1)} fusion(bf16[1,2560,1024]{2,1,0:T(8,128)(2,1)} %param.10, bf16[1,2560,1024]{2,1,0:T(8,128)(2,1)} %param.11), kind=kOutput, calls=%fused_computation.9 | convolution fusion | flops 5369757696 | bytes 12582912 | tf_op jit(solution)/shard_map/dot_general | solution.py:30
  16.6 4.7 %convolution_bitcast_fusion = f32[32,1024]{1,0:T(8,128)} fusion(f32[1,32,1024]{2,1,0:T(8,128)S(1)} %copy-done, f32[1,1,1024,1024]{3,2,1,0:T(8,128)S(1)} %copy-done.1, bf16[1024,1024]{1,0:T(8,128)(2,1)S(1)} %fusion.5), kind=kOutput, calls=%fused_computation.10 | convolution fusion | flops 404750336 | bytes 6553600 | tf_op jit(solution)/shard_map/dot_general | solution.py:39
  21.2 0.0 all-reduce.5.cloned.1.call-update
  21.3 0.0 all-reduce.7.cloned.1.call-start
  21.3 89.8 %all-reduce.5.cloned.1.call-done = f32[32,1024]{1,0:T(8,128)} async-done(((f32[32,1024]{1,0:T(8,128)}), f32[32,1024]{1,0:T(8,128)}) %all-reduce.5.cloned.1.call-update) | async-done | bytes 131088 | tf_op jit(solution)/shard_map/psum | solution.py:46
  111.1 1.8 multiply_reduce_fusion.1
  113.7 5.6 %fusion.15 = f32[32,1024]{1,0:T(8,128)} fusion(f32[1024,32]{0,1:T(8,128)S(1)} %get-tuple-element.10, f32[]{:T(128)S(6)} %rsqrt.7, f32[1,1,1024,1024]{3,2,1,0:T(8,128)} %param.12, bf16[1024,1024]{1,0:T(8,128)(2,1)S(1)} %fusion.5), kind=kOutput, calls=%fused_computation.20 | convolution fusion | flops 404783104 | bytes 6553604 | tf_op jit(solution)/shard_map/dot_general | solution.py:50
  119.2 0.0 all-reduce.7.cloned.1.call-update
  119.2 0.0 all-reduce.9.cloned.1.call-start
  119.3 36.2 %all-reduce.7.cloned.1.call-done = f32[32,1024]{1,0:T(8,128)} async-done(((f32[32,1024]{1,0:T(8,128)}), f32[32,1024]{1,0:T(8,128)}) %all-reduce.7.cloned.1.call-update) | async-done | bytes 131088 | tf_op jit(solution)/shard_map/psum | solution.py:51
  155.5 6.8 %fusion.13 = f32[32,1024]{1,0:T(8,128)} fusion(f32[32,1024]{1,0:T(8,128)} %all-reduce.7.cloned.1.call-done, f32[1,1,1024,1024]{3,2,1,0:T(8,128)} %param.12, bf16[1024,1024]{1,0:T(8,128)(2,1)S(1)} %fusion.5), kind=kOutput, calls=%fused_computation.18 | convolution fusion | flops 404783104 | bytes 6553600 | tf_op jit(solution)/shard_map/dot_general | solution.py:39
  162.3 0.2 all-reduce.11.cloned.1.call-start
  162.5 86.6 %all-reduce.9.cloned.1.call-done = f32[32,1024]{1,0:T(8,128)} async-done(((f32[32,1024]{1,0:T(8,128)}), f32[32,1024]{1,0:T(8,128)}) %all-reduce.9.cloned.1.call-update) | async-done | bytes 131088 | tf_op jit(solution)/shard_map/psum | solution.py:46
  249.1 1.8 multiply_reduce_fusion
  251.6 5.6 %fusion.23 = f32[32,1024]{1,0:T(8,128)} fusion(f32[1024,32]{0,1:T(8,128)S(1)} %get-tuple-element.12, f32[]{:T(128)S(6)} %rsqrt.8, f32[1,1,1024,1024]{3,2,1,0:T(8,128)} %param.12, bf16[1024,1024]{1,0:T(8,128)(2,1)S(1)} %fusion.5), kind=kOutput, calls=%fused_computation.30 | convolution fusion | flops 404783104 | bytes 6553604 | tf_op jit(solution)/shard_map/dot_general | solution.py:50
  257.3 0.0 all-gather.3.cloned.1.call-start
  257.3 0.2 fusion.20
  257.6 36.0 %all-reduce.11.cloned.1.call-done = f32[32,1024]{1,0:T(8,128)} async-done(((f32[32,1024]{1,0:T(8,128)}), f32[32,1024]{1,0:T(8,128)}) %all-reduce.11.cloned.1.call-update) | async-done | bytes 131088 | tf_op jit(solution)/shard_map/psum | solution.py:51
  293.6 1.8 fusion.11
  295.4 14.0 %psum.39 = f32[]{:T(128)} all-reduce(f32[]{:T(128)} %fusion.11), channel_id=1, replica_groups=mesh['shard'=4,'tensor'=4,'section'=2] {'tensor','section'}, use_global_device_ids=true, to_apply=%region_7.0 | all-reduce | flops 1 | bytes 8 | tf_op jit(solution)/shard_map/psum | solution.py:54
  310.1 4.5 %fusion.18 = f32[1024,1024]{1,0:T(8,128)S(1)} fusion(f32[32,1024]{1,0:T(8,128)} %all-reduce.11.cloned.1.call-done, f32[1024,32]{0,1:T(8,128)S(1)} %get-tuple-element.12, f32[]{:T(128)S(6)} %rsqrt.8), kind=kOutput, calls=%fused_computation.25 | convolution fusion | flops 402718720 | bytes 4456452 | tf_op jit(solution)/shard_map/dot_general | solution.py:55
  314.6 2.0 copy-done.3
  316.6 1.9 fusion.41
  318.6 18.6 %all-gather = s32[8,1,128]{2,1,0:T(1,128)S(1)} all-gather(s32[1,1,128]{2,1,0:T(1,128)S(1)} %bitcast.48), channel_id=1, replica_groups=mesh['shard'=4,'tensor'=4,'section'=2] {'shard','section'}, dimensions={0}, use_global_device_ids=true | all-gather | bytes 4608 | tf_op jit(solution)/shard_map/all_gather | solution.py:78
  337.2 33.2 %all_gather.11 = bf16[1024,256]{1,0:T(8,128)(2,1)S(1)} all-gather(bf16[128,256]{1,0:T(8,128)(2,1)S(1)} %copy-done.8), channel_id=1, replica_groups=mesh['shard'=4,'tensor'=4,'section'=2] {'shard','section'}, dimensions={0}, use_global_device_ids=true | all-gather | bytes 589824 | tf_op jit(solution)/shard_map/all_gather | solution.py:77
  370.3 8.3 %scatter_custom_fusion = f32[4096,256]{1,0:T(8,128)} fusion(s32[1024]{0:T(1024)S(1)} %compare_select_fusion, f32[]{:T(128)} %constant.16.clone.1, bf16[1024,256]{1,0:T(8,128)(2,1)S(1)} %all_gather.11), kind=kCustom, calls=%fused_computation.7 | custom fusion | flops 524288 | bytes 4718596 | tf_op jit(solution)/shard_map/scatter-add | solution.py:86
  378.6 4.8 %subtract_convert_fusion = bf16[4096,256]{1,0:T(8,128)(2,1)} fusion(f32[4096,256]{1,0:T(8,128)} %scatter_custom_fusion, bf16[4096,256]{1,0:T(8,128)(2,1)} %param.17), kind=kLoop, calls=%fused_computation.5 | loop fusion | flops 4194304 | bytes 8388608 | tf_op jit(solution)/shard_map/convert_element_type | solution.py:88
  383.4 0.7 multiply_bitcast_fusion
  384.1 0.6 copy-done.4
  384.7 3.6 subtract_bitcast_fusion
  388.3 3.1 copy.21
  (26 shorter events, 0.1 us)
Async XLA Ops:
  7.2 9.4 %copy-start = (f32[1,32,1024]{2,1,0:T(8,128)S(1)}, f32[1,32,1024]{2,1,0:T(8,128)}, u32[]{:S(2)}) copy-start(f32[1,32,1024]{2,1,0:T(8,128)} %param.13) | copy-start | bytes 393220
  7.2 103.9 %all-reduce.5.cloned.1.call-start = ((), (), s32[]{:S(2)}) async-start(), calls=%async_computation | async-start | bytes 262144 | tf_op jit(solution)/shard_map/psum | solution.py:46
  7.2 9.3 %copy-start.1 = (f32[1,1,1024,1024]{3,2,1,0:T(8,128)S(1)}, f32[1,1,1024,1024]{3,2,1,0:T(8,128)}, u32[]{:S(2)}) copy-start(f32[1,1,1024,1024]{3,2,1,0:T(8,128)} %param.12) | copy-start | bytes 12582916
  16.5 94.6 %copy-start.9 = (f32[1,2,32,32]{3,2,1,0:T(8,128)S(1)}, f32[1,2,32,32]{3,2,1,0:T(8,128)}, u32[]{:S(2)}) copy-start(f32[1,2,32,32]{3,2,1,0:T(8,128)} %param.14) | copy-start | bytes 24580
  21.3 134.2 %all-reduce.7.cloned.1.call-start = ((), (), s32[]{:S(2)}) async-start(), calls=%async_computation.1 | async-start | bytes 262144 | tf_op jit(solution)/shard_map/psum | solution.py:51
  119.2 129.8 %all-reduce.9.cloned.1.call-start = ((), (), s32[]{:S(2)}) async-start(), calls=%async_computation.2 | async-start | bytes 262144 | tf_op jit(solution)/shard_map/psum | solution.py:46
  162.3 131.3 %all-reduce.11.cloned.1.call-start = ((), (), s32[]{:S(2)}) async-start(), calls=%async_computation.3 | async-start | bytes 262144 | tf_op jit(solution)/shard_map/psum | solution.py:51
  251.6 65.0 %copy-start.6 = (f32[1,256,1024]{2,1,0:T(8,128)S(1)}, f32[1,256,1024]{2,1,0:T(8,128)}, u32[]{:S(2)}) copy-start(f32[1,256,1024]{2,1,0:T(8,128)} %param.16) | copy-start | bytes 3145732
  257.3 131.1 %all-gather.3.cloned.1.call-start = ((), (), s32[]{:S(2)}) async-start(), calls=%async_computation.4 | async-start | bytes 2621440 | tf_op jit(solution)/shard_map/all_gather | solution.py:71
  310.1 6.5 %copy-start.7 = (f32[1,256,1024]{2,1,0:T(8,128)S(1)}, f32[1,256,1024]{2,1,0:T(8,128)}, u32[]{:S(2)}) copy-start(f32[1,256,1024]{2,1,0:T(8,128)} %param.15) | copy-start | bytes 3145732
  314.6 2.0 copy-start.3
  316.6 2.0 copy-start.10
  316.6 20.6 %copy-start.8 = (bf16[128,256]{1,0:T(8,128)(2,1)S(1)}, bf16[128,256]{1,0:T(8,128)(2,1)}, u32[]{:S(2)}) copy-start(bf16[128,256]{1,0:T(8,128)(2,1)} %param.19) | copy-start | bytes 196612
  370.3 13.1 %copy-start.5 = (f32[32,1024]{1,0:T(8,128)S(1)}, f32[32,1024]{1,0:T(8,128)}, u32[]{:S(2)}) copy-start(f32[32,1024]{1,0:T(8,128)} %all-reduce.11.cloned.1.call-done) | copy-start | bytes 393220
  378.6 5.5 %copy-start.2 = (f32[1,1,1024,1024]{3,2,1,0:T(8,128)S(1)}, f32[1,1,1024,1024]{3,2,1,0:T(8,128)}, u32[]{:S(2)}) copy-start(f32[1,1,1024,1024]{3,2,1,0:T(8,128)} %param.12) | copy-start | bytes 12582916
  378.6 6.1 %copy-start.4 = (f32[1024,1024]{1,0:T(8,128)S(1)}, f32[1024,1024]{1,0:T(8,128)}, u32[]{:S(2)}) copy-start(f32[1024,1024]{1,0:T(8,128)} %copy-done.3) | copy-start | bytes 12582916
Sparse Core Ops, SparseCore 0:
  21.4 89.6 all-reduce.4
  119.4 36.0 all-reduce.6
  162.4 86.6 all-reduce.8
  257.4 36.1 all-reduce.10
  318.7 49.5 all-gather.2
where the time goes:
time: 398 us
  waiting for transfers between devices  249 us (63%)
  blocking collectives  65.7 us (17%)
  matrix products  42.2 us (11%)
  other arithmetic  19.3 us (5%)
  between operations  16 us (4%)
  local copies, waits for them, and re-layouts  5.77 us (1%)
    psum x2, waiting for transfers between devices, on_device(): left_sum = lax.psum(left_part, ('shard', 'tensor'))  176 us
    psum x2, waiting for transfers between devices, on_device(): right_part = lax.psum(right_local, 'shard') / shards  72.2 us
    all_gather x1, blocking collectives, on_device(): lax.all_gather(touched_grads, ('shard', 'section'), axis=0, tiled=True)  33.2 us
    all_gather x1, blocking collectives, on_device(): lax.all_gather(touched_ids, ('shard', 'section'), axis=0, tiled=True)  18.6 us
    psum x1, blocking collectives, on_device(): lax.psum(jnp.sum(gram_left * gram_right), ('tensor', 'section'))  14 us
    dot_general x2, matrix products, on_device(): lax.dot_general(right_part, corrected, (((1,), (1,)), ((), ())), precisio...  11.4 us
    dot_general x2, matrix products, on_device(): right_local = jnp.dot(left_unit, corrected, precision=highest)  11.2 us
    dot_general x1, matrix products, on_device(): lax.dot_general(out_grads[0], hidden_acts[0], (((0,), (0,)), ((), ())), p...  9.28 us
  transfers between devices with their start and end apart: 5, of which 4 were waited for; matrix products, arithmetic and copies ran while one was open for 4% of the time, Pallas kernels for 0%

commit v1 on v0

--- a/solution.py
+++ b/solution.py
@@ -12,6 +12,24 @@
 embed_rate = 0.25
 clip_level = 0.03
 highest = lax.Precision.HIGHEST
+
+
+def ring_gather(array, axis, dim):
+    ways, here, step = (lax.axis_size(axis), lax.axis_index(axis), array.shape[dim])
+    lengths = [n * ways if d == dim else n for d, n in enumerate(array.shape)]
+    full = lax.dynamic_update_slice_in_dim(
+        jnp.zeros(lengths, array.dtype), array, here * step, axis=dim
+    )
+    going_up = going_down = array
+    for far in range(1, ways // 2 + 1):
+        going_up = lax.ppermute(going_up, axis, [(d, (d + 1) % ways) for d in range(ways)])
+        full = lax.dynamic_update_slice_in_dim(full, going_up, (here - far) % ways * step, axis=dim)
+        if 2 * far < ways:
+            going_down = lax.ppermute(going_down, axis, [(d, (d - 1) % ways) for d in range(ways)])
+            full = lax.dynamic_update_slice_in_dim(
+                full, going_down, (here + far) % ways * step, axis=dim
+            )
+    return full
 
 
 def on_device(
@@ -75,7 +93,7 @@
     first_row = lax.axis_index(("shard", "section")) * vocab_rows
     recv_rows, recv_ids = (
         lax.all_gather(touched_grads, ("shard", "section"), axis=0, tiled=True),
-        lax.all_gather(touched_ids, ("shard", "section"), axis=0, tiled=True),
+        ring_gather(touched_ids, ("shard", "section"), 0),
     )
     local_index = recv_ids - first_row
     inside = (local_index >= 0) & (local_index < vocab_rows)

time: 398 us -> 403 us (1.013)
  blocking collectives: 65.7 us -> 47.1 us
  starting transfers between devices: 0.39 us -> 12.3 us
  waiting for transfers between devices: 249 us -> 258 us
    all_gather x1 -> x0, blocking collectives: 18.6 us -> none  [on_device(): lax.all_gather(touched_ids, ('shard', 'section'), axis=0, tiled=True)]
    ppermute x0 -> x7, starting transfers between devices: none -> 11.9 us  [the longest x3 10.1 us: ring_gather(): lax.ppermute(going_down, axis, [(d, (d - 1) % ways) for d in range(ways)])]
    ppermute x0 -> x7, waiting for transfers between devices: none -> 7.9 us  [the longest x4 7.89 us: ring_gather(): lax.ppermute(going_up, axis, [(d, (d + 1) % ways) for d in range(ways)])]
  transfers between devices with their start and end apart: 5 -> 12, of which waited for: 4 -> 7; matrix products, arithmetic and copies ran while one was open for 4% -> 5% of each run, Pallas kernels for 0% -> 0%
where the time goes in v1:
time: 403 us
  waiting for transfers between devices  258 us (64%)
  blocking collectives  47.1 us (12%)
  matrix products  42.1 us (10%)
  other arithmetic  19.3 us (5%)
  between operations  16 us (4%)
  starting transfers between devices  12.3 us (3%)
  local copies, waits for them, and re-layouts  7.37 us (2%)
    psum x2, waiting for transfers between devices, on_device(): left_sum = lax.psum(left_part, ('shard', 'tensor'))  179 us
    psum x2, waiting for transfers between devices, on_device(): right_part = lax.psum(right_local, 'shard') / shards  71 us
    all_gather x1, blocking collectives, on_device(): lax.all_gather(touched_grads, ('shard', 'section'), axis=0, tiled=True)  33.1 us
    psum x1, blocking collectives, on_device(): lax.psum(jnp.sum(gram_left * gram_right), ('tensor', 'section'))  14 us
    dot_general x2, matrix products, on_device(): right_local = jnp.dot(left_unit, corrected, precision=highest)  11.2 us
    dot_general x2, matrix products, on_device(): lax.dot_general(right_part, corrected, (((1,), (1,)), ((), ())), precisio...  10.9 us
    ppermute x3, starting transfers between devices, ring_gather(): lax.ppermute(going_down, axis, [(d, (d - 1) % ways) for d in range(ways)])  10.1 us
    dot_general x1, matrix products, on_device(): lax.dot_general(out_grads[0], hidden_acts[0], (((0,), (0,)), ((), ())), p...  9.28 us
  transfers between devices with their start and end apart: 12, of which 7 were waited for; matrix products, arithmetic and copies ran while one was open for 5% of the time, Pallas kernels for 0%

profile of v1, /device:TPU:0, one launch (start us, length us, event | category | flops | bytes accessed | tf_op | source)
XLA Modules:
  0.0 402.6 jit_solution(835239645425002063)
XLA Ops:
  7.2 9.3 %fusion.5 = bf16[1024,1024]{1,0:T(8,128)(2,1)S(1)} fusion(bf16[1,2560,1024]{2,1,0:T(8,128)(2,1)} %param.10, bf16[1,2560,1024]{2,1,0:T(8,128)(2,1)} %param.11), kind=kOutput, calls=%fused_computation.9 | convolution fusion | flops 5369757696 | bytes 12582912 | tf_op jit(solution)/shard_map/dot_general | solution.py:48
  16.6 4.2 %convolution_bitcast_fusion = f32[32,1024]{0,1:T(8,128)} fusion(f32[1,32,1024]{2,1,0:T(8,128)S(1)} %copy-done, f32[1,1,1024,1024]{3,2,1,0:T(8,128)S(1)} %copy-done.1, bf16[1024,1024]{1,0:T(8,128)(2,1)S(1)} %fusion.5), kind=kOutput, calls=%fused_computation.10 | convolution fusion | flops 404750336 | bytes 6553600 | tf_op jit(solution)/shard_map/dot_general | solution.py:57
  20.8 92.9 %all-reduce.5.cloned.1.call-done = f32[32,1024]{0,1:T(8,128)} async-done(((f32[32,1024]{0,1:T(8,128)}), f32[32,1024]{0,1:T(8,128)}) %all-reduce.5.cloned.1.call-update) | async-done | bytes 131088 | tf_op jit(solution)/shard_map/psum | solution.py:64
  113.7 2.3 multiply_reduce_fusion.1
  116.7 5.6 %fusion.15 = f32[32,1024]{1,0:T(8,128)} fusion(f32[1024,32]{0,1:T(8,128)S(1)} %get-tuple-element.10, f32[]{:T(128)S(6)} %rsqrt.7, f32[1,1,1024,1024]{3,2,1,0:T(8,128)} %param.12, bf16[1024,1024]{1,0:T(8,128)(2,1)S(1)} %fusion.5), kind=kOutput, calls=%fused_computation.20 | convolution fusion | flops 404783104 | bytes 6553604 | tf_op jit(solution)/shard_map/dot_general | solution.py:68
  122.3 35.0 %all-reduce.7.cloned.1.call-done = f32[32,1024]{1,0:T(8,128)} async-done(((f32[32,1024]{1,0:T(8,128)}), f32[32,1024]{1,0:T(8,128)}) %all-reduce.7.cloned.1.call-update) | async-done | bytes 131088 | tf_op jit(solution)/shard_map/psum | solution.py:69
  157.3 6.8 %fusion.13 = f32[32,1024]{1,0:T(8,128)} fusion(f32[32,1024]{1,0:T(8,128)} %all-reduce.7.cloned.1.call-done, f32[1,1,1024,1024]{3,2,1,0:T(8,128)} %param.12, bf16[1024,1024]{1,0:T(8,128)(2,1)S(1)} %fusion.5), kind=kOutput, calls=%fused_computation.18 | convolution fusion | flops 404783104 | bytes 6553600 | tf_op jit(solution)/shard_map/dot_general | solution.py:57
  164.1 0.2 all-reduce.11.cloned.1.call-start
  164.4 86.6 %all-reduce.9.cloned.1.call-done = f32[32,1024]{1,0:T(8,128)} async-done(((f32[32,1024]{1,0:T(8,128)}), f32[32,1024]{1,0:T(8,128)}) %all-reduce.9.cloned.1.call-update) | async-done | bytes 131088 | tf_op jit(solution)/shard_map/psum | solution.py:64
  251.0 1.8 multiply_reduce_fusion
  253.5 5.6 %fusion.23 = f32[32,1024]{1,0:T(8,128)} fusion(f32[1024,32]{0,1:T(8,128)S(1)} %get-tuple-element.12, f32[]{:T(128)S(6)} %rsqrt.8, f32[1,1,1024,1024]{3,2,1,0:T(8,128)} %param.12, bf16[1024,1024]{1,0:T(8,128)(2,1)S(1)} %fusion.5), kind=kOutput, calls=%fused_computation.30 | convolution fusion | flops 404783104 | bytes 6553604 | tf_op jit(solution)/shard_map/dot_general | solution.py:68
  259.2 0.2 fusion.20
  259.5 36.0 %all-reduce.11.cloned.1.call-done = f32[32,1024]{1,0:T(8,128)} async-done(((f32[32,1024]{1,0:T(8,128)}), f32[32,1024]{1,0:T(8,128)}) %all-reduce.11.cloned.1.call-update) | async-done | bytes 131088 | tf_op jit(solution)/shard_map/psum | solution.py:69
  295.5 1.8 fusion.11
  297.3 14.0 %psum.39 = f32[]{:T(128)} all-reduce(f32[]{:T(128)} %fusion.11), channel_id=1, replica_groups=mesh['shard'=4,'tensor'=4,'section'=2] {'tensor','section'}, use_global_device_ids=true, to_apply=%region_7.0 | all-reduce | flops 1 | bytes 8 | tf_op jit(solution)/shard_map/psum | solution.py:72
  312.0 4.5 %fusion.18 = f32[1024,1024]{1,0:T(8,128)S(1)} fusion(f32[32,1024]{1,0:T(8,128)} %all-reduce.11.cloned.1.call-done, f32[1024,32]{0,1:T(8,128)S(1)} %get-tuple-element.12, f32[]{:T(128)S(6)} %rsqrt.8), kind=kOutput, calls=%fused_computation.25 | convolution fusion | flops 402718720 | bytes 4456452 | tf_op jit(solution)/shard_map/dot_general | solution.py:73
  316.5 2.0 copy-done.3
  318.5 1.9 fusion.41
  320.5 2.4 collective-permute-start.1
  322.8 33.1 %all_gather.7 = bf16[1024,256]{1,0:T(8,128)(2,1)S(1)} all-gather(bf16[128,256]{1,0:T(8,128)(2,1)S(1)} %copy-done.8), channel_id=1, replica_groups=mesh['shard'=4,'tensor'=4,'section'=2] {'shard','section'}, dimensions={0}, use_global_device_ids=true | all-gather | bytes 589824 | tf_op jit(solution)/shard_map/all_gather | solution.py:95
  355.9 1.8 collective-permute-start.2
  357.7 3.0 collective-permute-start.3
  360.7 1.5 collective-permute-done.2
  362.2 4.8 %collective-permute-start.5 = (s32[128]{0:T(128)S(1)}, s32[128]{0:T(128)S(1)}, u32[]{:S(2)}, u32[]{:S(2)}) collective-permute-start(s32[128]{0:T(128)S(1)} %collective-permute-done.3), channel_id=1, source_target_pairs={{0,25},{1,0},{8,1},{9,8},{16,9},{17,16},{24,17},{25,24},{2,27},{3,... | collective-permute-start | bytes 1544 | tf_op jit(solution)/shard_map/ppermute | solution.py:28
  367.0 1.6 collective-permute-done.4
  370.0 4.8 %collective-permute-done.6 = s32[128]{0:T(128)S(1)} collective-permute-done((s32[128]{0:T(128)S(1)}, s32[128]{0:T(128)S(1)}, u32[]{:S(2)}, u32[]{:S(2)}) %collective-permute-start.6) | collective-permute-done | bytes 544 | tf_op jit(solution)/shard_map/ppermute | solution.py:25
  375.0 8.3 %scatter_custom_fusion = f32[4096,256]{1,0:T(8,128)} fusion(s32[1024]{0:T(1024)S(1)} %compare_select_fusion, f32[]{:T(128)} %constant.72.clone.1, bf16[1024,256]{1,0:T(8,128)(2,1)S(1)} %all_gather.7), kind=kCustom, calls=%fused_computation.7 | custom fusion | flops 524288 | bytes 4718596 | tf_op jit(solution)/shard_map/scatter-add | solution.py:104
  383.3 4.8 %subtract_convert_fusion = bf16[4096,256]{1,0:T(8,128)(2,1)} fusion(f32[4096,256]{1,0:T(8,128)} %scatter_custom_fusion, bf16[4096,256]{1,0:T(8,128)(2,1)} %param.17), kind=kLoop, calls=%fused_computation.5 | loop fusion | flops 4194304 | bytes 8388608 | tf_op jit(solution)/shard_map/convert_element_type | solution.py:106
  388.1 0.7 multiply_bitcast_fusion
  388.8 0.6 copy-done.4
  389.4 3.6 subtract_bitcast_fusion
  393.0 3.1 copy.29
  (47 shorter events, 1.9 us)
Async XLA Ops:
  7.2 9.4 %copy-start = (f32[1,32,1024]{2,1,0:T(8,128)S(1)}, f32[1,32,1024]{2,1,0:T(8,128)}, u32[]{:S(2)}) copy-start(f32[1,32,1024]{2,1,0:T(8,128)} %param.13) | copy-start | bytes 393220
  7.2 106.5 %all-reduce.5.cloned.1.call-start = ((), (), s32[]{:S(2)}) async-start(), calls=%async_computation | async-start | bytes 1048576 | tf_op jit(solution)/shard_map/psum | solution.py:64
  7.2 9.3 %copy-start.1 = (f32[1,1,1024,1024]{3,2,1,0:T(8,128)S(1)}, f32[1,1,1024,1024]{3,2,1,0:T(8,128)}, u32[]{:S(2)}) copy-start(f32[1,1,1024,1024]{3,2,1,0:T(8,128)} %param.12) | copy-start | bytes 12582916
  16.5 97.1 %copy-start.9 = (f32[1,2,32,32]{3,2,1,0:T(8,128)S(1)}, f32[1,2,32,32]{3,2,1,0:T(8,128)}, u32[]{:S(2)}) copy-start(f32[1,2,32,32]{3,2,1,0:T(8,128)} %param.14) | copy-start | bytes 24580
  20.8 136.6 %all-reduce.7.cloned.1.call-start = ((), (), s32[]{:S(2)}) async-start(), calls=%async_computation.1 | async-start | bytes 262144 | tf_op jit(solution)/shard_map/psum | solution.py:69
  122.3 128.7 %all-reduce.9.cloned.1.call-start = ((), (), s32[]{:S(2)}) async-start(), calls=%async_computation.2 | async-start | bytes 262144 | tf_op jit(solution)/shard_map/psum | solution.py:64
  164.1 131.4 %all-reduce.11.cloned.1.call-start = ((), (), s32[]{:S(2)}) async-start(), calls=%async_computation.3 | async-start | bytes 262144 | tf_op jit(solution)/shard_map/psum | solution.py:69
  253.5 65.0 %copy-start.6 = (f32[1,256,1024]{2,1,0:T(8,128)S(1)}, f32[1,256,1024]{2,1,0:T(8,128)}, u32[]{:S(2)}) copy-start(f32[1,256,1024]{2,1,0:T(8,128)} %param.16) | copy-start | bytes 3145732
  259.2 133.8 %all-gather.2.cloned.1.call-start = ((), (), s32[]{:S(2)}) async-start(), calls=%async_computation.4 | async-start | bytes 2621440 | tf_op jit(solution)/shard_map/all_gather | solution.py:89
  312.0 6.5 %copy-start.7 = (f32[1,256,1024]{2,1,0:T(8,128)S(1)}, f32[1,256,1024]{2,1,0:T(8,128)}, u32[]{:S(2)}) copy-start(f32[1,256,1024]{2,1,0:T(8,128)} %param.15) | copy-start | bytes 3145732
  316.5 2.0 copy-start.3
  318.5 1.9 copy-start.10
  318.5 4.3 %copy-start.8 = (bf16[128,256]{1,0:T(8,128)(2,1)S(1)}, bf16[128,256]{1,0:T(8,128)(2,1)}, u32[]{:S(2)}) copy-start(bf16[128,256]{1,0:T(8,128)(2,1)} %param.19) | copy-start | bytes 196612
  320.5 37.3 %collective-permute-start.1 = (s32[128]{0:T(128)S(1)}, s32[128]{0:T(128)S(1)}, u32[]{:S(2)}, u32[]{:S(2)}) collective-permute-start(s32[128]{0:T(128)S(1)} %copy-done.10), channel_id=1, source_target_pairs={{0,25},{1,0},{8,1},{9,8},{16,9},{17,16},{24,17},{25,24},{2,27},{3,... | collective-permute-start | bytes 1544 | tf_op jit(solution)/shard_map/ppermute | solution.py:28
  322.8 33.1 %collective-permute-start = (s32[128]{0:T(128)S(1)}, s32[128]{0:T(128)S(1)}, u32[]{:S(2)}, u32[]{:S(2)}) collective-permute-start(s32[128]{0:T(128)S(1)} %copy-done.10), channel_id=1, source_target_pairs={{0,1},{1,8},{8,9},{9,16},{16,17},{17,24},{24,25},{25,0},{2,3},{3,1... | collective-permute-start | bytes 1544 | tf_op jit(solution)/shard_map/ppermute | solution.py:25
  355.9 6.3 %collective-permute-start.2 = (s32[128]{0:T(128)S(1)}, s32[128]{0:T(128)S(1)}, u32[]{:S(2)}, u32[]{:S(2)}) collective-permute-start(s32[128]{0:T(128)S(1)} %collective-permute-done), channel_id=1, source_target_pairs={{0,1},{1,8},{8,9},{9,16},{16,17},{17,24},{24,25},{25,0},{2,3},{3,1... | collective-permute-start | bytes 1544 | tf_op jit(solution)/shard_map/ppermute | solution.py:25
  357.7 4.5 %collective-permute-start.3 = (s32[128]{0:T(128)S(1)}, s32[128]{0:T(128)S(1)}, u32[]{:S(2)}, u32[]{:S(2)}) collective-permute-start(s32[128]{0:T(128)S(1)} %collective-permute-done.1), channel_id=1, source_target_pairs={{0,25},{1,0},{8,1},{9,8},{16,9},{17,16},{24,17},{25,24},{2,27},{3,... | collective-permute-start | bytes 1544 | tf_op jit(solution)/shard_map/ppermute | solution.py:28
  362.2 6.3 %collective-permute-start.4 = (s32[128]{0:T(128)S(1)}, s32[128]{0:T(128)S(1)}, u32[]{:S(2)}, u32[]{:S(2)}) collective-permute-start(s32[128]{0:T(128)S(1)} %collective-permute-done.2), channel_id=1, source_target_pairs={{0,1},{1,8},{8,9},{9,16},{16,17},{17,24},{24,25},{25,0},{2,3},{3,1... | collective-permute-start | bytes 1544 | tf_op jit(solution)/shard_map/ppermute | solution.py:25
  362.2 7.6 %collective-permute-start.5 = (s32[128]{0:T(128)S(1)}, s32[128]{0:T(128)S(1)}, u32[]{:S(2)}, u32[]{:S(2)}) collective-permute-start(s32[128]{0:T(128)S(1)} %collective-permute-done.3), channel_id=1, source_target_pairs={{0,25},{1,0},{8,1},{9,8},{16,9},{17,16},{24,17},{25,24},{2,27},{3,... | collective-permute-start | bytes 1544 | tf_op jit(solution)/shard_map/ppermute | solution.py:28
  368.6 6.2 %collective-permute-start.6 = (s32[128]{0:T(128)S(1)}, s32[128]{0:T(128)S(1)}, u32[]{:S(2)}, u32[]{:S(2)}) collective-permute-start(s32[128]{0:T(128)S(1)} %collective-permute-done.4), channel_id=1, source_target_pairs={{0,1},{1,8},{8,9},{9,16},{16,17},{17,24},{24,25},{25,0},{2,3},{3,1... | collective-permute-start | bytes 1544 | tf_op jit(solution)/shard_map/ppermute | solution.py:25
  375.0 13.1 %copy-start.5 = (f32[32,1024]{1,0:T(8,128)S(1)}, f32[32,1024]{1,0:T(8,128)}, u32[]{:S(2)}) copy-start(f32[32,1024]{1,0:T(8,128)} %all-reduce.11.cloned.1.call-done) | copy-start | bytes 393220
  383.3 5.5 %copy-start.2 = (f32[1,1,1024,1024]{3,2,1,0:T(8,128)S(1)}, f32[1,1,1024,1024]{3,2,1,0:T(8,128)}, u32[]{:S(2)}) copy-start(f32[1,1,1024,1024]{3,2,1,0:T(8,128)} %param.12) | copy-start | bytes 12582916
  383.3 6.1 %copy-start.4 = (f32[1024,1024]{1,0:T(8,128)S(1)}, f32[1024,1024]{1,0:T(8,128)}, u32[]{:S(2)}) copy-start(f32[1024,1024]{1,0:T(8,128)} %copy-done.3) | copy-start | bytes 12582916
Sparse Core Ops, SparseCore 0:
  20.9 92.7 all-reduce.4
  122.4 34.8 all-reduce.6
  164.2 86.6 all-reduce.8
  259.3 36.1 all-reduce.10
  320.6 48.7 all-gather.1
